TPU v7x, 512 devices: a whole 4x8x8 slice. The times are simulated.
512 devices in a mesh: station: 32 (over y, x), tm: 16 (over z, core).
Axes of the slice: x: 4, y: 8, z: 8, core: 2. Of those that a mesh axis runs over, the one named last changes fastest.
Arguments:
- spectra: bfloat16 [16, 128, 4096], P('tm', 'station'), may hold values from -5 to 5
- valid: int32 [16, 128], P('tm', 'station'), may hold values from 0 to 1, as said below
- pair_blocks: int32 [32, 17], P('station'), may hold values from 0 to 31, as said below
Outputs:
- correlations: float32 [8704, 512], P(('station', 'tm'))
Inputs may be any that keep to these rules, and one draw needn't show every extreme that they name: `pair_blocks`: row d begins with d, its 17 entries are distinct, and every unordered pair of blocks appears in some row. `valid`: each station misses one cyclic run of 1 to 7 hours.
All inputs are finite; a program needn't handle non-finite values.
Results may differ from a plain program's by a relative error of at most 0.0026.
Values may be sent and summed in bfloat16 or wider, within the bound.
A program may use at most 64 MiB of HBM per device.

v0:
```python
import math
import jax
import jax.numpy as jnp
from jax import lax
from jax.sharding import PartitionSpec as P

LAGS = 512


def make_lag_table(half_width, lag_count):
    bins = jnp.arange(half_width, dtype=jnp.int32)
    shifts = jnp.arange(lag_count, dtype=jnp.int32) - lag_count // 2
    phase = (2 * bins[:, None] + 1) * shifts[None, :] % (4 * half_width)
    angle = phase.astype(jnp.float32) * (math.pi / (2.0 * half_width))
    return jnp.concatenate([jnp.cos(angle), -jnp.sin(angle)], axis=0).astype(jnp.bfloat16)


def cross_stack(own_block, partner_block, half_width):
    own_real, own_imag = (own_block[..., :half_width], own_block[..., half_width:])
    part_real, part_imag = (partner_block[..., :half_width], partner_block[..., half_width:])
    cross_real = jnp.einsum(
        "haf,hkbf->kabf", own_real, part_real, preferred_element_type=jnp.float32
    ) + jnp.einsum("haf,hkbf->kabf", own_imag, part_imag, preferred_element_type=jnp.float32)
    cross_imag = jnp.einsum(
        "haf,hkbf->kabf", own_imag, part_real, preferred_element_type=jnp.float32
    ) - jnp.einsum("haf,hkbf->kabf", own_real, part_imag, preferred_element_type=jnp.float32)
    return jnp.concatenate([cross_real, cross_imag], axis=-1).astype(jnp.bfloat16)


def per_device(spectra, valid, pair_blocks):
    local_hours, block_len, spec_width = spectra.shape
    half_width = spec_width // 2
    lag_count = LAGS
    stations_axis = lax.axis_size("station")
    slot_count = pair_blocks.shape[1]
    plan = pair_blocks[0]
    masked = spectra * valid[:, :, None].astype(jnp.bfloat16)
    gathered, gathered_flags = (
        lax.all_gather(masked, "station", axis=1, tiled=True),
        lax.all_gather(valid, "station", axis=1, tiled=True),
    )
    gathered = gathered.reshape(local_hours, stations_axis, block_len, spec_width)
    gathered_flags = gathered_flags.reshape(local_hours, stations_axis, block_len)
    partners = jnp.take(gathered, plan, axis=1)
    partner_flags = jnp.take(gathered_flags, plan, axis=1)
    per_slot = block_len * block_len
    pair_count = slot_count * per_slot
    lag_table = make_lag_table(half_width, lag_count)
    stacked = cross_stack(masked, partners, half_width).reshape(pair_count, spec_width)
    partial_value = jnp.dot(stacked, lag_table, preferred_element_type=jnp.float32)
    local_counts = jnp.einsum(
        "ha,hkb->kab", valid.astype(jnp.float32), partner_flags.astype(jnp.float32)
    ).reshape(pair_count)
    summed, counts = (
        lax.psum_scatter(partial_value, "tm", scatter_dimension=0, tiled=True),
        lax.psum_scatter(local_counts, "tm", scatter_dimension=0, tiled=True),
    )
    lag_scale = 4.0 / math.sqrt(half_width)
    return summed * lag_scale / counts[:, None]


def solution(mesh):
    placed = (P("tm", "station", None), P("tm", "station"), P("station", None))
    return jax.shard_map(
        per_device,
        mesh=mesh,
        in_specs=placed,
        out_specs=P(("station", "tm"), None),
        check_vma=False,
    )
```

profile of v0, /device:TPU:1, one launch (start us, length us, event | category | flops | bytes accessed | tf_op | source)
XLA Modules:
  0.0 195.7 jit_solution(14837320123272706570)
XLA Ops:
  6.5 0.0 all-gather.2.cloned.1.call-start
  6.5 0.7 convert_bitcast_fusion.2
  7.3 1.5 copy_multiply_fusion
  8.8 0.0 all-gather.2.cloned.1.call-update
  8.8 0.7 compare_and_fusion
  9.5 0.7 fusion.16
  10.1 1.3 dynamic-slice
  12.1 0.8 bitcast_dynamic-update-slice_fusion
  12.8 17.5 %all-reduce = s32[128]{0:T(128)S(1)} all-reduce(s32[128]{0:T(128)S(1)} %bitcast_dynamic-update-slice_fusion), channel_id=1, replica_groups=mesh['station'=32,'tm'=16] {'station'}, use_global_device_ids=true, to_apply=%add | all-reduce | flops 128 | bytes 1024
  30.3 0.1 reshape.171
  30.4 0.6 gather_fusion.1
  31.0 0.1 copy.16
  31.1 0.1 copy.17
  31.2 0.8 slice_convert_fusion.1
  32.0 19.2 %cosine_convert_fusion = (bf16[2048,512]{1,0:T(8,128)(2,1)}, bf16[2048,512]{1,0:T(8,128)(2,1)}) fusion(s32[512]{0:T(512)S(1)} %iota_add_fusion, s32[2048]{0:T(1024)S(1)} %multiply_add_fusion), kind=kLoop, calls=%fused_computation.15 | loop fusion | flops 17825792 | bytes 4204544 | tf_op jit(solution)/shard_map/convert.24
  51.2 44.4 %all-gather.2.cloned.1.call-done = bf16[1,128,4096]{2,0,1:T(2,128)(2,1)} async-done(((bf16[1,4,4096]{2,0,1:T(2,128)(2,1)}), bf16[1,128,4096]{2,0,1:T(2,128)(2,1)}) %all-gather.2.cloned.1.call-update) | async-done | bytes 1048592 | tf_op jit(solution)/shard_map/all_gather | solution.py:39
  95.6 7.7 %reduce = bf16[128,4096]{1,0:T(8,128)(2,1)S(1)} reduce(bf16[1,128,4096]{2,0,1:T(2,128)(2,1)} %all-gather.2.cloned.1.call-done, bf16[]{:T(256)} %constant.71), dimensions={0}, to_apply=%all_gather.6.reduce_sub_computation | reduce | bytes 2097154 | tf_op jit(solution)/shard_map/all_gather | solution.py:39
  103.3 0.4 reshape.161
  103.8 1.0 gather_fusion
  104.8 0.3 bitcast_select_fusion
  105.1 0.1 convert_bitcast_fusion.1
  105.2 1.2 fusion.11
  106.4 1.2 concatenate.13
  107.6 0.0 copy-start
  107.6 1.1 concatenate.14
  108.7 0.9 copy-done
  109.6 0.0 copy-start.1
  109.6 3.6 %fusion.4 = f32[272,512]{1,0:T(8,128)S(1)} fusion(bf16[2048,512]{1,0:T(8,128)(2,1)} %get-tuple-element.12, bf16[2048,512]{1,0:T(8,128)(2,1)S(1)} %copy-done, bf16[272,2048]{1,0:T(8,128)(2,1)} %concatenate.14, bf16[272,2048]{1,0:T(8,128)(2,1)} %concatenate.13), kind=kOutput, calls=%fused_computation.10 | convolution fusion | flops 1153695744 | bytes 6979584 | tf_op jit(solution)/shard_map/dot_general | solution.py:50
  113.2 32.3 %fusion = f32[24,512]{1,0:T(8,128)S(1)} fusion(f32[272,512]{1,0:T(8,128)S(1)} %fusion.4), kind=kCustom, calls=%all-reduce-scatter | all-reduce-scatter fusion | flops 196609 | bytes 608256
  145.5 1.5 collective-permute-start.3
  146.9 9.1 %collective-permute-start.2 = (f32[24,512]{1,0:T(8,128)S(1)}, f32[24,512]{1,0:T(8,128)S(1)}, u32[]{:S(2)}, u32[]{:S(2)}) collective-permute-start(f32[24,512]{1,0:T(8,128)S(1)} %fusion), channel_id=1, source_target_pairs={{0,3},{1,4},{2,5},{3,6},{4,7},{5,8},{6,9},{7,10},{8,11},{9,12},{10... | collective-permute-start | bytes 147464
  156.0 1.3 collective-permute-start.1
  157.3 3.1 %collective-permute-start = (f32[24,512]{1,0:T(8,128)S(1)}, f32[24,512]{1,0:T(8,128)S(1)}, u32[]{:S(2)}, u32[]{:S(2)}) collective-permute-start(f32[24,512]{1,0:T(8,128)S(1)} %fusion), channel_id=1, source_target_pairs={{0,1},{1,2},{2,3},{3,4},{4,5},{5,6},{6,7},{7,8},{8,9},{9,10},{10,1... | collective-permute-start | bytes 147464
  160.4 1.4 collective-permute-start.4
  161.8 0.1 multiply_bitcast_fusion
  161.8 0.1 reshape.156
  162.0 0.0 copy-done.1
  162.0 0.6 fusion.18
  163.8 23.6 %all-reduce.2 = f32[272]{0:T(512)S(1)} all-reduce(f32[272]{0:T(512)S(1)} %reshape.156), channel_id=3, replica_groups=mesh['station'=32,'tm'=16] {'tm'}, use_global_device_ids=true, to_apply=%region_1.2.clone | all-reduce | flops 272 | bytes 2176
  187.3 0.1 dynamic-slice.4
  187.4 0.0 collective-permute-done.4
  187.4 0.0 collective-permute-done.3
  187.4 0.0 collective-permute-done.2
  187.4 0.0 collective-permute-done.1
  187.4 0.0 collective-permute-done
  187.5 0.7 concatenate.17
  188.2 0.7 fusion.13
  (7 shorter events, 0.1 us)
Async XLA Ops:
  6.5 89.0 %all-gather.2.cloned.1.call-start = ((), (), s32[]{:S(2)}) async-start(), calls=%async_computation | async-start | bytes 2162688 | tf_op jit(solution)/shard_map/all_gather | solution.py:39
  107.6 2.0 %copy-start = (bf16[2048,512]{1,0:T(8,128)(2,1)S(1)}, bf16[2048,512]{1,0:T(8,128)(2,1)}, u32[]{:S(2)}) copy-start(bf16[2048,512]{1,0:T(8,128)(2,1)} %get-tuple-element.11) | copy-start | bytes 6291460
  109.6 52.4 %copy-start.1 = (u32[512]{0:T(512)S(1)}, u32[512]{0:T(512)}, u32[]{:S(2)}) copy-start(u32[512]{0:T(512)} %constant.65) | copy-start | bytes 6148
  145.5 42.0 %collective-permute-start.3 = (f32[24,512]{1,0:T(8,128)S(1)}, f32[24,512]{1,0:T(8,128)S(1)}, u32[]{:S(2)}, u32[]{:S(2)}) collective-permute-start(f32[24,512]{1,0:T(8,128)S(1)} %fusion), channel_id=1, source_target_pairs={{0,4},{1,5},{2,6},{3,7},{4,8},{5,9},{6,10},{7,11},{8,12},{9,13},{1... | collective-permute-start | bytes 147464
  146.9 40.5 %collective-permute-start.2 = (f32[24,512]{1,0:T(8,128)S(1)}, f32[24,512]{1,0:T(8,128)S(1)}, u32[]{:S(2)}, u32[]{:S(2)}) collective-permute-start(f32[24,512]{1,0:T(8,128)S(1)} %fusion), channel_id=1, source_target_pairs={{0,3},{1,4},{2,5},{3,6},{4,7},{5,8},{6,9},{7,10},{8,11},{9,12},{10... | collective-permute-start | bytes 147464
  156.0 31.5 %collective-permute-start.1 = (f32[24,512]{1,0:T(8,128)S(1)}, f32[24,512]{1,0:T(8,128)S(1)}, u32[]{:S(2)}, u32[]{:S(2)}) collective-permute-start(f32[24,512]{1,0:T(8,128)S(1)} %fusion), channel_id=1, source_target_pairs={{0,2},{1,3},{2,4},{3,5},{4,6},{5,7},{6,8},{7,9},{8,10},{9,11},{10,... | collective-permute-start | bytes 147464
  157.3 30.2 %collective-permute-start = (f32[24,512]{1,0:T(8,128)S(1)}, f32[24,512]{1,0:T(8,128)S(1)}, u32[]{:S(2)}, u32[]{:S(2)}) collective-permute-start(f32[24,512]{1,0:T(8,128)S(1)} %fusion), channel_id=1, source_target_pairs={{0,1},{1,2},{2,3},{3,4},{4,5},{5,6},{6,7},{7,8},{8,9},{9,10},{10,1... | collective-permute-start | bytes 147464
  160.4 27.0 %collective-permute-start.4 = (f32[9,512]{1,0:T(8,128)S(1)}, f32[9,512]{1,0:T(8,128)S(1)}, u32[]{:S(2)}, u32[]{:S(2)}) collective-permute-start(f32[9,512]{1,0:T(8,128)S(1)} %slice.24), channel_id=1, source_target_pairs={{0,5},{1,6},{2,7},{3,8},{4,9},{5,10},{6,11},{7,12},{8,13},{9,14},{... | collective-permute-start | bytes 55304
Sparse Core Ops, SparseCore 0:
  10.5 85.0 all-gather.1
where the time goes:
time: 196 us
  blocking collectives  73.3 us (37%)
  waiting for transfers between devices  44.4 us (23%)
  other arithmetic  33.7 us (17%)
  starting transfers between devices  16.3 us (8%)
  between operations  15.5 us (8%)
  local copies, waits for them, and re-layouts  9.01 us (5%)
  matrix products  3.59 us (2%)
    unnamed x3, blocking collectives  73.3 us
    all_gather x1, waiting for transfers between devices, per_device(): lax.all_gather(masked, 'station', axis=1, tiled=True)  44.4 us
    another operation x4, other arithmetic  20.9 us
    unnamed x5, starting transfers between devices  16.3 us
    all_gather x1, other arithmetic, per_device(): lax.all_gather(masked, 'station', axis=1, tiled=True)  7.73 us
    unnamed x11, local copies, waits for them, and re-layouts  4.29 us
  transfers between devices with their start and end apart: 6, of which 1 were waited for; matrix products, arithmetic and copies ran while one was open for 13% of the time, Pallas kernels for 0%

commit v1 on v0

--- a/solution.py
+++ b/solution.py
@@ -5,6 +5,14 @@
 from jax.sharding import PartitionSpec as P
 
 LAGS = 512
+
+
+def tiled_gather(array, axis, dim):
+    size = lax.axis_size(axis)
+    repeats = [size if d == dim else 1 for d in range(array.ndim)]
+    return lax.all_to_all(
+        jnp.tile(array, repeats), axis, split_axis=dim, concat_axis=dim, tiled=True
+    )
 
 
 def make_lag_table(half_width, lag_count):
@@ -36,7 +44,7 @@
     plan = pair_blocks[0]
     masked = spectra * valid[:, :, None].astype(jnp.bfloat16)
     gathered, gathered_flags = (
-        lax.all_gather(masked, "station", axis=1, tiled=True),
+        tiled_gather(masked, "station", 1),
         lax.all_gather(valid, "station", axis=1, tiled=True),
     )
     gathered = gathered.reshape(local_hours, stations_axis, block_len, spec_width)

time: 196 us -> 169 us (0.86)
  waiting for transfers between devices: 44.4 us -> 0.02 us
  blocking collectives: 73.3 us -> 87.5 us
  between operations: 15.5 us -> 2.23 us
  local copies, waits for them, and re-layouts: 9.01 us -> 19.8 us
  starting transfers between devices: 16.3 us -> 24.9 us
  other arithmetic: 33.7 us -> 30.3 us
    all_gather x1 -> x0, waiting for transfers between devices: 44.4 us -> none  [per_device(): lax.all_gather(masked, 'station', axis=1, tiled=True)]
    unnamed x3, blocking collectives: 73.3 us -> 87.5 us
    all_to_all x0 -> x1, starting transfers between devices: none -> 10.5 us  [tiled_gather(): lax.all_to_all(jnp.tile(array, repeats), axis, split_axis=dim, concat_axi...]
    all_gather x1 -> x0, other arithmetic: 7.73 us -> none  [per_device(): lax.all_gather(masked, 'station', axis=1, tiled=True)]
    unnamed x0 -> x1, other arithmetic: none -> 7.02 us
    all_to_all x0 -> x1, local copies, waits for them, and re-layouts: none -> 6.21 us  [tiled_gather(): lax.all_to_all(jnp.tile(array, repeats), axis, split_axis=dim, concat_axi...]
    unnamed x11 -> x20, local copies, waits for them, and re-layouts: 4.29 us -> 6.9 us
    another operation x1 -> x2, local copies, waits for them, and re-layouts: 0.03 us -> 2.01 us  [tiled_gather(): jnp.tile(array, repeats)]
  transfers between devices with their start and end apart: 6 -> 6, of which waited for: 1 -> 0; matrix products, arithmetic and copies ran while one was open for 13% -> 13% of each run, Pallas kernels for 0% -> 0%
where the time goes in v1:
time: 169 us; the launch traced here: 168 us
  blocking collectives  87.5 us (52%)
  other arithmetic  30.3 us (18%)
  starting transfers between devices  24.9 us (15%)
  local copies, waits for them, and re-layouts  19.8 us (12%)
  matrix products  3.59 us (2%)
  between operations  2.23 us (1%)
    unnamed x3, blocking collectives  87.5 us
    another operation x4, other arithmetic  20 us
    unnamed x5, starting transfers between devices  14.4 us
    all_to_all x1, starting transfers between devices, tiled_gather(): lax.all_to_all(jnp.tile(array, repeats), axis, split_axis=dim, concat_axi...  10.5 us
    unnamed x1, other arithmetic  7.02 us
    unnamed x20, local copies, waits for them, and re-layouts  6.9 us
    all_to_all x1, local copies, waits for them, and re-layouts, tiled_gather(): lax.all_to_all(jnp.tile(array, repeats), axis, split_axis=dim, concat_axi...  6.21 us
    dot_general x1, matrix products, per_device(): jnp.dot(stacked, lag_table, preferred_element_type=jnp.float32)  3.59 us
  transfers between devices with their start and end apart: 6, of which 0 were waited for; matrix products, arithmetic and copies ran while one was open for 13% of the time, Pallas kernels for 0%

profile of v1, /device:TPU:1, one launch (start us, length us, event | category | flops | bytes accessed | tf_op | source)
XLA Modules:
  0.0 168.3 jit_solution(15026225264998155883)
XLA Ops:
  0.0 0.7 convert_bitcast_fusion.4
  0.7 0.8 fusion.19
  1.6 0.5 tile.12
  2.1 1.5 tile.14
  3.6 0.5 broadcast.142
  4.1 7.0 %reduce.2 = bf16[128,4096]{1,0:T(8,128)(2,1)S(1)} reduce(bf16[128,1,4096]{2,1,0:T(2,128)(2,1)S(1)} %bitcast.65, bf16[]{:T(256)} %broadcast.142), dimensions={1}, to_apply=%bitcast.61.reduce_sub_computation | reduce | bytes 2097154
  11.1 0.0 copy-start.3
  11.2 0.0 copy-start.4
  11.2 0.0 copy-start.1
  11.2 1.6 reshape.199
  12.8 10.5 %all-to-all-start = ((bf16[32,2,8192]{2,1,0:T(2,128)(2,1)}), bf16[32,2,8192]{2,1,0:T(2,128)(2,1)S(1)}, u32[]{:S(2)}, u32[]{:S(2)}) async-start(bf16[32,2,8192]{2,1,0:T(2,128)(2,1)} %reshape.199), calls=%async_computation | async-start | bytes 2097152 | tf_op jit(solution)/shard_map/all_to_all | solution.py:13
  23.4 1.3 dynamic-slice
  25.3 0.1 bitcast_dynamic-update-slice_fusion
  25.4 28.7 %all-reduce = s32[128]{0:T(128)S(1)} all-reduce(s32[128]{0:T(128)S(1)} %bitcast_dynamic-update-slice_fusion), channel_id=1, replica_groups=mesh['station'=32,'tm'=16] {'station'}, use_global_device_ids=true, to_apply=%add | all-reduce | flops 128 | bytes 1024
  54.1 0.1 reshape.177
  54.2 0.6 gather_fusion.1
  54.8 0.1 copy.15
  54.9 0.1 copy.16
  55.0 0.1 broadcast_multiply_fusion
  55.1 19.2 %cosine_convert_fusion = (bf16[2048,512]{1,0:T(8,128)(2,1)}, bf16[2048,512]{1,0:T(8,128)(2,1)}) fusion(s32[512]{0:T(512)S(1)} %iota_add_fusion, s32[2048]{0:T(1024)S(1)} %multiply_add_fusion), kind=kLoop, calls=%fused_computation.15 | loop fusion | flops 17825792 | bytes 4204544 | tf_op jit(solution)/shard_map/convert.24
  74.3 0.0 all-to-all-done
  74.3 1.1 reshape.200
  75.4 6.2 %bitcast_reduce_fusion = bf16[128,4096]{1,0:T(8,128)(2,1)S(1)} fusion(bf16[128,1,4096]{2,1,0:T(2,128)(2,1)S(1)} %reshape.200), kind=kLoop, calls=%fused_computation.51 | loop fusion | bytes 2097152 | tf_op jit(solution)/shard_map/all_to_all | solution.py:13
  81.6 0.4 reshape.167
  82.0 1.0 gather_fusion
  83.0 0.3 bitcast_select_fusion
  83.4 0.1 convert_bitcast_fusion.1
  83.5 1.2 fusion.11
  84.7 1.2 concatenate.13
  85.8 1.1 concatenate.14
  87.0 0.9 copy-done
  87.8 3.6 %fusion.4 = f32[272,512]{1,0:T(8,128)S(1)} fusion(bf16[2048,512]{1,0:T(8,128)(2,1)} %get-tuple-element.12, bf16[2048,512]{1,0:T(8,128)(2,1)S(1)} %copy-done, bf16[272,2048]{1,0:T(8,128)(2,1)} %concatenate.14, bf16[272,2048]{1,0:T(8,128)(2,1)} %concatenate.13), kind=kOutput, calls=%fused_computation.10 | convolution fusion | flops 1153695744 | bytes 6979584 | tf_op jit(solution)/shard_map/dot_general | solution.py:58
  91.4 35.2 %fusion = f32[24,512]{1,0:T(8,128)S(1)} fusion(f32[272,512]{1,0:T(8,128)S(1)} %fusion.4), kind=kCustom, calls=%all-reduce-scatter | all-reduce-scatter fusion | flops 196609 | bytes 608256
  126.7 1.3 collective-permute-start.3
  128.0 7.0 %collective-permute-start.2 = (f32[24,512]{1,0:T(8,128)S(1)}, f32[24,512]{1,0:T(8,128)S(1)}, u32[]{:S(2)}, u32[]{:S(2)}) collective-permute-start(f32[24,512]{1,0:T(8,128)S(1)} %fusion), channel_id=1, source_target_pairs={{0,3},{1,4},{2,5},{3,6},{4,7},{5,8},{6,9},{7,10},{8,11},{9,12},{10... | collective-permute-start | bytes 147464
  135.0 1.3 collective-permute-start.1
  136.3 3.1 %collective-permute-start = (f32[24,512]{1,0:T(8,128)S(1)}, f32[24,512]{1,0:T(8,128)S(1)}, u32[]{:S(2)}, u32[]{:S(2)}) collective-permute-start(f32[24,512]{1,0:T(8,128)S(1)} %fusion), channel_id=1, source_target_pairs={{0,1},{1,2},{2,3},{3,4},{4,5},{5,6},{6,7},{7,8},{8,9},{9,10},{10,1... | collective-permute-start | bytes 147464
  139.4 1.7 collective-permute-start.4
  141.1 0.1 multiply_bitcast_fusion
  141.2 0.1 reshape.162
  141.3 0.6 fusion.18
  143.2 23.6 %all-reduce.2 = f32[272]{0:T(512)S(1)} all-reduce(f32[272]{0:T(512)S(1)} %reshape.162), channel_id=3, replica_groups=mesh['station'=32,'tm'=16] {'tm'}, use_global_device_ids=true, to_apply=%region_1.2.clone | all-reduce | flops 272 | bytes 2176
  166.8 0.1 dynamic-slice.4
  166.8 0.0 collective-permute-done.4
  166.9 0.0 collective-permute-done.3
  166.9 0.0 collective-permute-done
  166.9 0.7 concatenate.17
  167.6 0.7 fusion.13
  (17 shorter events, 0.1 us)
Async XLA Ops:
  11.1 12.2 %copy-start.3 = (s32[1,17]{1,0:T(1,128)S(1)}, s32[1,17]{1,0:T(1,128)}, u32[]{:S(2)}) copy-start(s32[1,17]{1,0:T(1,128)} %param.5) | copy-start | bytes 208
  11.2 14.2 %copy-start.4 = (s32[1,4]{1,0:T(1,128)S(1)}, s32[1,4]{1,0:T(1,128)}, u32[]{:S(2)}) copy-start(s32[1,4]{1,0:T(1,128)} %param.4) | copy-start | bytes 52
  11.2 43.8 %copy-start.1 = (bf16[1,4,4096]{2,1,0:T(4,128)(2,1)S(1)}, bf16[1,4,4096]{2,1,0:T(4,128)(2,1)}, u32[]{:S(2)}) copy-start(bf16[1,4,4096]{2,1,0:T(4,128)(2,1)} %param.3) | copy-start | bytes 98308
  12.8 61.5 %all-to-all-start = ((bf16[32,2,8192]{2,1,0:T(2,128)(2,1)}), bf16[32,2,8192]{2,1,0:T(2,128)(2,1)S(1)}, u32[]{:S(2)}, u32[]{:S(2)}) async-start(bf16[32,2,8192]{2,1,0:T(2,128)(2,1)} %reshape.199), calls=%async_computation | async-start | bytes 2097152 | tf_op jit(solution)/shard_map/all_to_all | solution.py:13
  85.8 2.0 %copy-start = (bf16[2048,512]{1,0:T(8,128)(2,1)S(1)}, bf16[2048,512]{1,0:T(8,128)(2,1)}, u32[]{:S(2)}) copy-start(bf16[2048,512]{1,0:T(8,128)(2,1)} %get-tuple-element.11) | copy-start | bytes 6291460
  87.8 53.5 %copy-start.2 = (u32[512]{0:T(512)S(1)}, u32[512]{0:T(512)}, u32[]{:S(2)}) copy-start(u32[512]{0:T(512)} %constant.65) | copy-start | bytes 6148
  126.7 40.2 %collective-permute-start.3 = (f32[24,512]{1,0:T(8,128)S(1)}, f32[24,512]{1,0:T(8,128)S(1)}, u32[]{:S(2)}, u32[]{:S(2)}) collective-permute-start(f32[24,512]{1,0:T(8,128)S(1)} %fusion), channel_id=1, source_target_pairs={{0,4},{1,5},{2,6},{3,7},{4,8},{5,9},{6,10},{7,11},{8,12},{9,13},{1... | collective-permute-start | bytes 147464
  128.0 38.9 %collective-permute-start.2 = (f32[24,512]{1,0:T(8,128)S(1)}, f32[24,512]{1,0:T(8,128)S(1)}, u32[]{:S(2)}, u32[]{:S(2)}) collective-permute-start(f32[24,512]{1,0:T(8,128)S(1)} %fusion), channel_id=1, source_target_pairs={{0,3},{1,4},{2,5},{3,6},{4,7},{5,8},{6,9},{7,10},{8,11},{9,12},{10... | collective-permute-start | bytes 147464
  135.0 31.8 %collective-permute-start.1 = (f32[24,512]{1,0:T(8,128)S(1)}, f32[24,512]{1,0:T(8,128)S(1)}, u32[]{:S(2)}, u32[]{:S(2)}) collective-permute-start(f32[24,512]{1,0:T(8,128)S(1)} %fusion), channel_id=1, source_target_pairs={{0,2},{1,3},{2,4},{3,5},{4,6},{5,7},{6,8},{7,9},{8,10},{9,11},{10,... | collective-permute-start | bytes 147464
  136.3 30.6 %collective-permute-start = (f32[24,512]{1,0:T(8,128)S(1)}, f32[24,512]{1,0:T(8,128)S(1)}, u32[]{:S(2)}, u32[]{:S(2)}) collective-permute-start(f32[24,512]{1,0:T(8,128)S(1)} %fusion), channel_id=1, source_target_pairs={{0,1},{1,2},{2,3},{3,4},{4,5},{5,6},{6,7},{7,8},{8,9},{9,10},{10,1... | collective-permute-start | bytes 147464
  139.4 27.4 %collective-permute-start.4 = (f32[9,512]{1,0:T(8,128)S(1)}, f32[9,512]{1,0:T(8,128)S(1)}, u32[]{:S(2)}, u32[]{:S(2)}) collective-permute-start(f32[9,512]{1,0:T(8,128)S(1)} %slice.24), channel_id=1, source_target_pairs={{0,5},{1,6},{2,7},{3,8},{4,9},{5,10},{6,11},{7,12},{8,13},{9,14},{... | collective-permute-start | bytes 55304
